TPU v7x, 256 devices: a whole 4x4x8 slice. The times are simulated.
256 devices in a mesh: snap: 8 (over z), py: 4 (over y_lo, core), pz: 8 (over y_hi, x).
Axes of the slice: x: 4, y: 4 (y_hi: 2, y_lo: 2; y = y_hi * 2 + y_lo), z: 8, core: 2. Of those that a mesh axis runs over, the one named last changes fastest.
Arguments:
- velocity: bfloat16 [8, 3, 48, 384, 1024], P('snap', None, 'pz', 'py'), may hold values from -6 to 6
- metric_x: float32 [1024], replicated, may hold values from 0.5 to 2
- metric_y: float32 [384], replicated, may hold values from 0.3 to 3
- metric_z: float32 [48], replicated, may hold values from 0.5 to 2
- sketch_matrix: float32 [8, 4], replicated, may hold values from -2 to 2
Outputs:
- sketch: float32 [4, 3, 48, 384, 1024], P(None, None, None, ('snap', 'pz'), 'py')
All inputs are finite; a program needn't handle non-finite values.
Results may differ from a plain program's by a relative error of at most 0.0065.
Values may be sent and summed in bfloat16 or wider, within the bound.
A program may use at most 128 MiB of HBM per device.

v0:
```python
import jax
import jax.numpy as jnp
from jax import lax
from jax.sharding import PartitionSpec as P

log_ratio = jnp.log((3.0 - 5.0**0.5) / 2.0)
scale_const = 5.0**0.5 / 3.0


def inverse_entry(row_index, col_index, length):
    inside = (col_index >= 0) & (col_index < length)
    column = jnp.clip(col_index, 0, length - 1)
    nearer = jnp.minimum(row_index, column).astype(jnp.float32)
    farther = jnp.maximum(row_index, column).astype(jnp.float32)
    distance = farther - nearer
    parity_sign = 1.0 - 2.0 * jnp.mod(distance, 2.0)
    magnitude = jnp.exp(distance * log_ratio) * parity_sign
    left_factor = 1.0 - jnp.exp(2.0 * (nearer + 1.0) * log_ratio)
    right_factor = 1.0 - jnp.exp(2.0 * (length - farther) * log_ratio)
    denominator = scale_const * (1.0 - jnp.exp(2.0 * (length + 1.0) * log_ratio))
    return jnp.where(inside, magnitude * left_factor * right_factor / denominator, 0.0)


def compact_table(length):
    row_index = lax.broadcasted_iota(jnp.int32, (length, length), 0)
    col_index = lax.broadcasted_iota(jnp.int32, (length, length), 1)
    first = inverse_entry(row_index, col_index - 1, length) - inverse_entry(
        row_index, col_index + 1, length
    )
    second = inverse_entry(row_index, col_index - 2, length) - inverse_entry(
        row_index, col_index + 2, length
    )
    return 7.0 / 9.0 * first + 1.0 / 36.0 * second


def split_table(length):
    table = compact_table(length)
    table_high = table.astype(jnp.bfloat16)
    table_low = (table - table_high.astype(jnp.float32)).astype(jnp.bfloat16)
    return (table_high, table_low)


def apply_split(form, tables, fields, table_first):
    table_high, table_low = tables
    if table_first:
        high_part = jnp.einsum(form, table_high, fields, preferred_element_type=jnp.float32)
        low_part = jnp.einsum(form, table_low, fields, preferred_element_type=jnp.float32)
    else:
        high_part = jnp.einsum(form, fields, table_high, preferred_element_type=jnp.float32)
        low_part = jnp.einsum(form, fields, table_low, preferred_element_type=jnp.float32)
    return high_part + low_part


def vorticity_from(zlines, metric_z):
    tables_z = split_table(zlines.shape[2])
    z_slopes = apply_split("ij,scjyx->sciyx", tables_z, zlines[:, 0:2], True)
    z_slopes = z_slopes * metric_z[None, None, :, None, None]
    slope_uz = z_slopes[:, 0]
    slope_vz = z_slopes[:, 1]
    slope_wx = zlines[:, 2].astype(jnp.float32)
    slope_wy = zlines[:, 3].astype(jnp.float32)
    spin_x = (slope_wy - slope_vz).astype(jnp.bfloat16)
    spin_y = (slope_uz - slope_wx).astype(jnp.bfloat16)
    return jnp.stack([spin_x, spin_y, zlines[:, 4]], axis=1)


def on_device(velocity, metric_x, metric_y, metric_z, sketch_matrix):
    tables_x = split_table(velocity.shape[4])
    x_slopes = apply_split("sczyj,ij->sczyi", tables_x, velocity[:, 1:3], False)
    x_slopes = (x_slopes * metric_x).astype(jnp.bfloat16)
    payload = jnp.concatenate([velocity, x_slopes], axis=1)
    ylines = lax.all_to_all(payload, "py", split_axis=4, concat_axis=3, tiled=True)
    tables_y = split_table(ylines.shape[3])
    y_slopes = apply_split("ij,sczjx->sczix", tables_y, ylines[:, 0:3:2], True)
    y_slopes = y_slopes * metric_y[None, None, None, :, None]
    slope_uy = y_slopes[:, 0]
    slope_wy = y_slopes[:, 1].astype(jnp.bfloat16)
    spin_z = (ylines[:, 3].astype(jnp.float32) - slope_uy).astype(jnp.bfloat16)
    z_payload = jnp.stack([ylines[:, 0], ylines[:, 1], ylines[:, 4], slope_wy, spin_z], axis=1)
    zlines = lax.all_to_all(
        lax.all_to_all(z_payload, "snap", split_axis=3, concat_axis=0, tiled=True),
        "pz",
        split_axis=3,
        concat_axis=2,
        tiled=True,
    )
    vorticity = vorticity_from(zlines, metric_z)
    return jnp.einsum(
        "sk,sczyx->kczyx",
        sketch_matrix,
        vorticity.astype(jnp.float32),
        precision=lax.Precision.HIGHEST,
    )


def solution(mesh):
    placed = (P("snap", None, "pz", "py", None), P(), P(), P(), P())
    return jax.shard_map(
        on_device,
        mesh=mesh,
        in_specs=placed,
        out_specs=P(None, None, None, ("snap", "pz"), "py"),
        check_vma=False,
    )
```

profile of v0, /device:TPU:30, one launch (start us, length us, event | category | flops | bytes accessed | tf_op | source)
XLA Modules:
  0.0 559.7 jit_solution(15133581711998774805)
XLA Ops:
  0.0 0.0 copy-start
  0.0 0.6 fusion.361
  0.6 0.6 fusion.367
  1.2 0.6 fusion.369
  1.8 8.1 %copy.36 = bf16[1,3,6,96,1024]{3,2,1,0,4:T(8,128)(2,1)} copy(bf16[1,3,6,96,1024]{4,3,2,1,0:T(8,128)(2,1)} %param.6) | data formatting | bytes 7077888 | tf_op args[0]
  9.9 0.0 copy-done.2
  9.9 0.0 copy-start.6
  9.9 0.0 copy-start.7
  9.9 0.0 copy-start.8
  10.0 0.0 copy-start.10
  10.0 29.3 %fusion.112 = f32[1024,2,6,96]{0,3,2,1:T(8,128)S(1)} fusion(s32[1024]{0:T(1024)S(1)} %get-tuple-element.12, s32[1024]{0:T(1024)S(1)} %get-tuple-element.13, s32[1024]{0:T(1024)S(1)} %get-tuple-element.14, s32[1024]{0:T(1024)} %get-tuple-element.15, pred[1024]{0:T(1024)(128)(4,1)} %get-tuple-element.19, pred[1024]{0:T(1024)(128)(4,1)} %get-tuple-element.18, ...), kind=kOutput, calls=%fused_computation.135 | convolution fusion | flops 2530213888 | bytes 7098368 | tf_op jit(solution)/shard_map/sczyj,ij->sczyi/dot_general | solution.py:50
  39.3 0.0 copy-done.3
  39.3 0.0 copy-done.5
  39.3 0.0 copy-done.6
  39.3 0.0 copy-done.7
  39.3 0.0 copy-done.8
  39.3 0.0 copy-done.10
  39.3 28.4 %fusion.104 = bf16[1,2,6,96,1024]{4,3,2,1,0:T(8,128)(2,1)} fusion(f32[1024,2,6,96]{0,3,2,1:T(8,128)S(1)} %fusion.112, f32[1024]{0:T(1024)S(1)} %copy-done.10, bf16[1,3,6,96,1024]{4,3,2,1,0:T(8,128)(2,1)S(1)} %copy-done.2, s32[1024]{0:T(1024)S(1)} %get-tuple-element.12, pred[1024]{0:T(1024)(128)(4,1)S(1)} %copy-done.8, s32[1024]{0:T(1024)S(1)} %get-tuple-element.13, ...), kind=kOutput, calls=%fused_computation.123 | convolution fusion | flops 2530607104 | bytes 9461760 | tf_op jit(solution)/shard_map/sczyj,ij->sczyi/dot_general | solution.py:49
  67.7 6.5 %copy.37 = bf16[1,2,6,96,1024]{3,2,1,0,4:T(8,128)(2,1)} copy(bf16[1,2,6,96,1024]{4,3,2,1,0:T(8,128)(2,1)} %fusion.104) | data formatting | bytes 4718592 | tf_op jit(solution)/shard_map/convert_element_type | solution.py:70
  74.2 10.8 %pad_maximum_fusion = bf16[1,5,6,96,1024]{3,2,1,0,4:T(8,128)(2,1)} fusion(bf16[1,2,6,96,1024]{3,2,1,0,4:T(8,128)(2,1)} %copy.37, bf16[1,3,6,96,1024]{3,2,1,0,4:T(8,128)(2,1)} %copy.36), kind=kLoop, calls=%fused_computation | loop fusion | flops 2949120 | bytes 11796480 | tf_op jit(solution)/shard_map/concatenate | solution.py:71
  85.0 6.8 %all-to-all-start = ((bf16[1,5,6,96,1024]{3,2,1,0,4:T(8,128)(2,1)}), bf16[1,5,6,96,1024]{3,2,1,0,4:T(8,128)(2,1)}, u32[]{:S(2)}, u32[]{:S(2)}) async-start(bf16[1,5,6,96,1024]{3,2,1,0,4:T(8,128)(2,1)} %pad_maximum_fusion), calls=%async_computation | async-start | bytes 20971520 | tf_op jit(solution)/shard_map/all_to_all | solution.py:72
  91.8 0.6 fusion.384
  92.4 0.6 fusion.386
  92.9 0.6 fusion.378
  93.5 112.3 %all-to-all-done = bf16[1,5,6,96,1024]{3,2,1,0,4:T(8,128)(2,1)} async-done(((bf16[1,5,6,96,1024]{3,2,1,0,4:T(8,128)(2,1)}), bf16[1,5,6,96,1024]{3,2,1,0,4:T(8,128)(2,1)}, u32[]{:S(2)}, u32[]{:S(2)}) %all-to-all-start) | async-done | bytes 5898272 | tf_op jit(solution)/shard_map/all_to_all | solution.py:72
  205.8 12.4 %copy.62 = bf16[1,5,6,96,4,256]{5,4,3,2,1,0:T(4,128)(2,1)} copy(bf16[1,5,6,96,4,256]{3,2,1,5,4,0:T(8,128)(2,1)} %bitcast.7) | data formatting | bytes 11796480 | tf_op jit(solution)/shard_map/all_to_all | solution.py:72
  218.2 3.9 copy.39
  222.0 0.0 copy-start.1
  222.0 1.7 fusion.447
  223.7 0.2 slice.55
  223.9 1.4 copy-done.1
  225.3 1.7 copy.66
  227.0 0.0 copy-start.4
  227.0 0.0 copy-start.11
  227.0 0.0 copy-start.12
  227.1 6.2 %fusion.108 = f32[2,6,256,384]{3,2,1,0:T(8,128)S(1)} fusion(bf16[1,5,6,384,256]{4,3,2,1,0:T(8,128)(2,1)} %bitcast.84, s32[384]{0:T(512)S(1)} %get-tuple-element.20, s32[384]{0:T(512)S(1)} %get-tuple-element.21, s32[384]{0:T(512)S(1)} %get-tuple-element.22, s32[384]{0:T(512)} %get-tuple-element.23, pred[384]{0:T(512)(128)(4,1)} %get-tuple-element.27, ...), kind=kOutput, calls=%fused_computation.131 | convolution fusion | flops 922042368 | bytes 7086592 | tf_op jit(solution)/shard_map/ij,sczjx->sczix/dot_general | solution.py:47
  233.3 0.0 copy-done.4
  233.3 0.0 copy-done.11
  233.3 0.0 copy-done.12
  233.3 0.0 copy-done.13
  233.4 0.0 copy-done.14
  233.4 0.0 copy-done.15
  233.4 6.4 %fusion = f32[1,2,6,384,256]{3,4,2,1,0:T(8,128)S(1)} fusion(f32[2,6,256,384]{3,2,1,0:T(8,128)S(1)} %fusion.108, f32[384]{0:T(512)S(1)} %copy-done.11, bf16[1,5,6,384,256]{4,3,2,1,0:T(8,128)(2,1)} %bitcast.85, s32[384]{0:T(512)S(1)} %get-tuple-element.20, pred[384]{0:T(512)(128)(4,1)S(1)} %copy-done.15, s32[384]{0:T(512)S(1)} %get-tuple-element.21, ...), kind=kOutput, calls=%fused_computation.15 | convolution fusion | flops 923959296 | bytes 11805696 | tf_op jit(solution)/shard_map/ij,sczjx->sczix/dot_general | solution.py:46
  239.8 1.2 slice.94
  240.9 1.4 fusion.107
  242.3 1.6 copy.43
  243.9 2.4 copy.42
  246.2 4.8 pad_maximum_fusion.1
  251.0 6.2 %copy.44 = bf16[1,5,6,384,256]{4,2,1,0,3:T(8,128)(2,1)S(1)} copy(bf16[1,5,6,384,256]{4,3,2,1,0:T(8,128)(2,1)} %pad_maximum_fusion.1) | data formatting | bytes 11796480 | tf_op jit(solution)/shard_map/stack | solution.py:79
  257.2 183.2 %all_to_all.54 = bf16[1,5,6,384,256]{4,2,1,0,3:T(8,128)(2,1)} all-to-all(bf16[1,5,6,384,256]{4,2,1,0,3:T(8,128)(2,1)S(1)} %copy.44), channel_id=1, replica_groups=mesh['snap'=8,'py'=4,'pz'=8] {'snap'}, dimensions={3} | all-to-all | bytes 11796480 | tf_op jit(solution)/shard_map/all_to_all | solution.py:81
  440.4 12.2 %copy.46 = bf16[8,5,6,48,256]{4,0,2,1,3:T(8,128)(2,1)} copy(bf16[8,5,6,48,256]{4,2,1,3,0:T(8,128)(2,1)} %bitcast.78) | data formatting | bytes 11796480 | tf_op jit(solution)/shard_map/all_to_all | solution.py:81
  452.7 7.5 %all-to-all-start.2 = ((bf16[8,5,6,48,256]{4,0,2,1,3:T(8,128)(2,1)}), bf16[8,5,6,48,256]{4,0,2,1,3:T(8,128)(2,1)}, u32[]{:S(2)}, u32[]{:S(2)}) async-start(bf16[8,5,6,48,256]{4,0,2,1,3:T(8,128)(2,1)} %copy.46), calls=%async_computation.2 | async-start | bytes 11796480 | tf_op jit(solution)/shard_map/all_to_all | solution.py:80
  460.2 81.9 %all-to-all-done.2 = bf16[8,5,6,48,256]{4,0,2,1,3:T(8,128)(2,1)} async-done(((bf16[8,5,6,48,256]{4,0,2,1,3:T(8,128)(2,1)}), bf16[8,5,6,48,256]{4,0,2,1,3:T(8,128)(2,1)}, u32[]{:S(2)}, u32[]{:S(2)}) %all-to-all-start.2) | async-done | bytes 5898272 | tf_op jit(solution)/shard_map/all_to_all | solution.py:80
  542.1 3.3 copy.48
  545.4 0.2 slice.61
  545.6 0.2 fusion.446
  545.8 0.4 copy.70
  546.3 0.0 copy-start.9
  546.3 2.1 fusion.123
  548.4 2.2 multiply_bitcast_fusion
  550.6 1.3 fusion.106
  551.9 0.4 pad_maximum_fusion.2
  552.4 4.0 fusion.130
  556.4 2.9 copy.54
  (14 shorter events, 0.1 us)
Async XLA Ops:
  0.0 552.4 %copy-start = (f32[8,4]{0,1:T(4,128)S(1)}, f32[8,4]{0,1:T(4,128)}, u32[]{:S(2)}) copy-start(f32[8,4]{0,1:T(4,128)} %param.10) | copy-start | bytes 388
  1.8 8.1 %copy-start.2 = (bf16[1,3,6,96,1024]{4,3,2,1,0:T(8,128)(2,1)S(1)}, bf16[1,3,6,96,1024]{4,3,2,1,0:T(8,128)(2,1)}, u32[]{:S(2)}) copy-start(bf16[1,3,6,96,1024]{4,3,2,1,0:T(8,128)(2,1)} %param.6) | copy-start | bytes 10616836
  9.9 29.3 %copy-start.3 = (s32[1024]{0:T(1024)S(1)}, s32[1024]{0:T(1024)}, u32[]{:S(2)}) copy-start(s32[1024]{0:T(1024)} %get-tuple-element.15) | copy-start | bytes 12292
  9.9 29.3 %copy-start.5 = (pred[1024]{0:T(1024)(128)(4,1)S(1)}, pred[1024]{0:T(1024)(128)(4,1)}, u32[]{:S(2)}) copy-start(pred[1024]{0:T(1024)(128)(4,1)} %get-tuple-element.16) | copy-start | bytes 3076
  9.9 29.4 %copy-start.6 = (pred[1024]{0:T(1024)(128)(4,1)S(1)}, pred[1024]{0:T(1024)(128)(4,1)}, u32[]{:S(2)}) copy-start(pred[1024]{0:T(1024)(128)(4,1)} %get-tuple-element.17) | copy-start | bytes 3076
  9.9 29.4 %copy-start.7 = (pred[1024]{0:T(1024)(128)(4,1)S(1)}, pred[1024]{0:T(1024)(128)(4,1)}, u32[]{:S(2)}) copy-start(pred[1024]{0:T(1024)(128)(4,1)} %get-tuple-element.18) | copy-start | bytes 3076
  9.9 29.4 %copy-start.8 = (pred[1024]{0:T(1024)(128)(4,1)S(1)}, pred[1024]{0:T(1024)(128)(4,1)}, u32[]{:S(2)}) copy-start(pred[1024]{0:T(1024)(128)(4,1)} %get-tuple-element.19) | copy-start | bytes 3076
  10.0 29.4 %copy-start.10 = (f32[1024]{0:T(1024)S(1)}, f32[1024]{0:T(1024)}, u32[]{:S(2)}) copy-start(f32[1024]{0:T(1024)} %param.7) | copy-start | bytes 12292
  85.0 120.8 %all-to-all-start = ((bf16[1,5,6,96,1024]{3,2,1,0,4:T(8,128)(2,1)}), bf16[1,5,6,96,1024]{3,2,1,0,4:T(8,128)(2,1)}, u32[]{:S(2)}, u32[]{:S(2)}) async-start(bf16[1,5,6,96,1024]{3,2,1,0,4:T(8,128)(2,1)} %pad_maximum_fusion), calls=%async_computation | async-start | bytes 20971520 | tf_op jit(solution)/shard_map/all_to_all | solution.py:72
  222.0 3.3 copy-start.1
  227.0 6.3 %copy-start.4 = (s32[384]{0:T(512)S(1)}, s32[384]{0:T(512)}, u32[]{:S(2)}) copy-start(s32[384]{0:T(512)} %get-tuple-element.23) | copy-start | bytes 4612
  227.0 6.3 %copy-start.11 = (f32[384]{0:T(512)S(1)}, f32[384]{0:T(512)}, u32[]{:S(2)}) copy-start(f32[384]{0:T(512)} %param.8) | copy-start | bytes 4612
  227.0 6.3 %copy-start.12 = (pred[384]{0:T(512)(128)(4,1)S(1)}, pred[384]{0:T(512)(128)(4,1)}, u32[]{:S(2)}) copy-start(pred[384]{0:T(512)(128)(4,1)} %get-tuple-element.24) | copy-start | bytes 1156
  227.0 6.3 %copy-start.13 = (pred[384]{0:T(512)(128)(4,1)S(1)}, pred[384]{0:T(512)(128)(4,1)}, u32[]{:S(2)}) copy-start(pred[384]{0:T(512)(128)(4,1)} %get-tuple-element.25) | copy-start | bytes 1156
  227.0 6.3 %copy-start.14 = (pred[384]{0:T(512)(128)(4,1)S(1)}, pred[384]{0:T(512)(128)(4,1)}, u32[]{:S(2)}) copy-start(pred[384]{0:T(512)(128)(4,1)} %get-tuple-element.26) | copy-start | bytes 1156
  227.0 6.3 %copy-start.15 = (pred[384]{0:T(512)(128)(4,1)S(1)}, pred[384]{0:T(512)(128)(4,1)}, u32[]{:S(2)}) copy-start(pred[384]{0:T(512)(128)(4,1)} %get-tuple-element.27) | copy-start | bytes 1156
  452.7 89.5 %all-to-all-start.2 = ((bf16[8,5,6,48,256]{4,0,2,1,3:T(8,128)(2,1)}), bf16[8,5,6,48,256]{4,0,2,1,3:T(8,128)(2,1)}, u32[]{:S(2)}, u32[]{:S(2)}) async-start(bf16[8,5,6,48,256]{4,0,2,1,3:T(8,128)(2,1)} %copy.46), calls=%async_computation.2 | async-start | bytes 11796480 | tf_op jit(solution)/shard_map/all_to_all | solution.py:80
  546.3 2.1 copy-start.9
where the time goes:
time: 571 us; the launch traced here: 560 us
  waiting for transfers between devices  194 us (34%)
  blocking collectives  183 us (32%)
  matrix products  78.6 us (14%)
  local copies, waits for them, and re-layouts  66.3 us (12%)
  other arithmetic  22.2 us (4%)
  starting transfers between devices  14.2 us (2%)
    all_to_all x1, blocking collectives, on_device(): lax.all_to_all(z_payload, 'snap', split_axis=3, concat_axis=0, tiled=True)  183 us
    all_to_all x1, waiting for transfers between devices, on_device(): lax.all_to_all(payload, 'py', split_axis=4, concat_axis=3, tiled=True)  112 us
    all_to_all x1, waiting for transfers between devices, on_device(): lax.all_to_all(lax.all_to_all(z_payload, 'snap', split_axis=3, concat_axi...  81.9 us
    dot_general x1, matrix products, apply_split(): jnp.einsum(form, fields, table_low, preferred_element_type=jnp.float32)  29.3 us
    dot_general x1, matrix products, apply_split(): jnp.einsum(form, fields, table_high, preferred_element_type=jnp.float32)  28.4 us
    all_to_all x2, local copies, waits for them, and re-layouts, on_device(): lax.all_to_all(payload, 'py', split_axis=4, concat_axis=3, tiled=True)  16.2 us
    all_to_all x1, local copies, waits for them, and re-layouts, on_device(): lax.all_to_all(z_payload, 'snap', split_axis=3, concat_axis=0, tiled=True)  12.2 us
    unnamed x35, local copies, waits for them, and re-layouts  11.7 us
  transfers between devices with their start and end apart: 2, of which 2 were waited for; matrix products, arithmetic and copies ran while one was open for 0% of the time, Pallas kernels for 0%

commit v1 on v0

--- a/solution.py
+++ b/solution.py
@@ -5,6 +5,12 @@
 
 log_ratio = jnp.log((3.0 - 5.0**0.5) / 2.0)
 scale_const = 5.0**0.5 / 3.0
+
+
+def stacked_exchange(value, mesh_axis, split, join):
+    cells = jnp.split(value, lax.axis_size(mesh_axis), axis=split)
+    received = lax.all_to_all(jnp.stack(cells), mesh_axis, 0, 0)
+    return jnp.concatenate(received, axis=join)
 
 
 def inverse_entry(row_index, col_index, length):
@@ -77,12 +83,8 @@
     slope_wy = y_slopes[:, 1].astype(jnp.bfloat16)
     spin_z = (ylines[:, 3].astype(jnp.float32) - slope_uy).astype(jnp.bfloat16)
     z_payload = jnp.stack([ylines[:, 0], ylines[:, 1], ylines[:, 4], slope_wy, spin_z], axis=1)
-    zlines = lax.all_to_all(
-        lax.all_to_all(z_payload, "snap", split_axis=3, concat_axis=0, tiled=True),
-        "pz",
-        split_axis=3,
-        concat_axis=2,
-        tiled=True,
+    zlines = stacked_exchange(
+        lax.all_to_all(z_payload, "snap", split_axis=3, concat_axis=0, tiled=True), "pz", 3, 2
     )
     vorticity = vorticity_from(zlines, metric_z)
     return jnp.einsum(

time: 571 us -> 570 us (level)
    all_to_all x1, local copies, waits for them, and re-layouts: 12.2 us -> 4.64 us  [on_device(): lax.all_to_all(z_payload, 'snap', split_axis=3, concat_axis=0, tiled=True)]
    unnamed x35 -> x42, local copies, waits for them, and re-layouts: 11.7 us -> 13.4 us
where the time goes in v1:
time: 570 us; the launch traced here: 559 us
  waiting for transfers between devices  194 us (34%)
  blocking collectives  183 us (32%)
  matrix products  78.7 us (14%)
  local copies, waits for them, and re-layouts  65.6 us (12%)
  other arithmetic  22.2 us (4%)
  starting transfers between devices  14.2 us (2%)
    all_to_all x1, blocking collectives, on_device(): lax.all_to_all(z_payload, 'snap', split_axis=3, concat_axis=0, tiled=True)  183 us
    all_to_all x1, waiting for transfers between devices, on_device(): lax.all_to_all(payload, 'py', split_axis=4, concat_axis=3, tiled=True)  112 us
    all_to_all x1, waiting for transfers between devices, stacked_exchange(): received = lax.all_to_all(jnp.stack(cells), mesh_axis, 0, 0)  81.9 us
    dot_general x1, matrix products, apply_split(): jnp.einsum(form, fields, table_low, preferred_element_type=jnp.float32)  29.3 us
    dot_general x1, matrix products, apply_split(): jnp.einsum(form, fields, table_high, preferred_element_type=jnp.float32)  28.4 us
    all_to_all x2, local copies, waits for them, and re-layouts, on_device(): lax.all_to_all(payload, 'py', split_axis=4, concat_axis=3, tiled=True)  16.2 us
    unnamed x42, local copies, waits for them, and re-layouts  13.4 us
  transfers between devices with their start and end apart: 2, of which 2 were waited for; matrix products, arithmetic and copies ran while one was open for 0% of the time, Pallas kernels for 0%

profile of v1, /device:TPU:30, one launch (start us, length us, event | category | flops | bytes accessed | tf_op | source)
XLA Modules:
  0.0 559.1 jit_solution(3593045733525880347)
XLA Ops:
  0.0 0.0 copy-start
  0.0 0.6 fusion.369
  0.6 0.6 fusion.375
  1.2 0.6 fusion.377
  1.8 8.1 %copy.34 = bf16[1,3,6,96,1024]{3,2,1,0,4:T(8,128)(2,1)} copy(bf16[1,3,6,96,1024]{4,3,2,1,0:T(8,128)(2,1)} %param.6) | data formatting | bytes 7077888 | tf_op args[0]
  9.9 0.0 copy-done.2
  9.9 0.0 copy-start.6
  9.9 0.0 copy-start.7
  10.0 0.0 copy-start.10
  10.0 29.3 %fusion.112 = f32[1024,2,6,96]{0,3,2,1:T(8,128)S(1)} fusion(s32[1024]{0:T(1024)S(1)} %get-tuple-element.12, s32[1024]{0:T(1024)S(1)} %get-tuple-element.13, s32[1024]{0:T(1024)S(1)} %get-tuple-element.14, s32[1024]{0:T(1024)} %get-tuple-element.15, pred[1024]{0:T(1024)(128)(4,1)} %get-tuple-element.19, pred[1024]{0:T(1024)(128)(4,1)} %get-tuple-element.18, ...), kind=kOutput, calls=%fused_computation.135 | convolution fusion | flops 2530213888 | bytes 7098368 | tf_op jit(solution)/shard_map/sczyj,ij->sczyi/dot_general | solution.py:56
  39.3 28.4 %fusion.104 = bf16[1,2,6,96,1024]{4,3,2,1,0:T(8,128)(2,1)} fusion(f32[1024,2,6,96]{0,3,2,1:T(8,128)S(1)} %fusion.112, f32[1024]{0:T(1024)S(1)} %copy-done.10, bf16[1,3,6,96,1024]{4,3,2,1,0:T(8,128)(2,1)S(1)} %copy-done.2, s32[1024]{0:T(1024)S(1)} %get-tuple-element.12, pred[1024]{0:T(1024)(128)(4,1)S(1)} %copy-done.8, s32[1024]{0:T(1024)S(1)} %get-tuple-element.13, ...), kind=kOutput, calls=%fused_computation.123 | convolution fusion | flops 2530607104 | bytes 9461760 | tf_op jit(solution)/shard_map/sczyj,ij->sczyi/dot_general | solution.py:55
  67.7 6.5 %copy.35 = bf16[1,2,6,96,1024]{3,2,1,0,4:T(8,128)(2,1)} copy(bf16[1,2,6,96,1024]{4,3,2,1,0:T(8,128)(2,1)} %fusion.104) | data formatting | bytes 4718592 | tf_op jit(solution)/shard_map/convert_element_type | solution.py:76
  74.2 10.8 %pad_maximum_fusion = bf16[1,5,6,96,1024]{3,2,1,0,4:T(8,128)(2,1)} fusion(bf16[1,2,6,96,1024]{3,2,1,0,4:T(8,128)(2,1)} %copy.35, bf16[1,3,6,96,1024]{3,2,1,0,4:T(8,128)(2,1)} %copy.34), kind=kLoop, calls=%fused_computation | loop fusion | flops 2949120 | bytes 11796480 | tf_op jit(solution)/shard_map/concatenate | solution.py:77
  85.0 6.8 %all-to-all-start = ((bf16[1,5,6,96,1024]{3,2,1,0,4:T(8,128)(2,1)}), bf16[1,5,6,96,1024]{3,2,1,0,4:T(8,128)(2,1)}, u32[]{:S(2)}, u32[]{:S(2)}) async-start(bf16[1,5,6,96,1024]{3,2,1,0,4:T(8,128)(2,1)} %pad_maximum_fusion), calls=%async_computation | async-start | bytes 20971520 | tf_op jit(solution)/shard_map/all_to_all | solution.py:78
  91.8 0.6 fusion.392
  92.4 0.6 fusion.394
  92.9 0.6 fusion.386
  93.5 112.3 %all-to-all-done = bf16[1,5,6,96,1024]{3,2,1,0,4:T(8,128)(2,1)} async-done(((bf16[1,5,6,96,1024]{3,2,1,0,4:T(8,128)(2,1)}), bf16[1,5,6,96,1024]{3,2,1,0,4:T(8,128)(2,1)}, u32[]{:S(2)}, u32[]{:S(2)}) %all-to-all-start) | async-done | bytes 5898272 | tf_op jit(solution)/shard_map/all_to_all | solution.py:78
  205.8 12.4 %copy.59 = bf16[1,5,6,96,4,256]{5,4,3,2,1,0:T(4,128)(2,1)} copy(bf16[1,5,6,96,4,256]{3,2,1,5,4,0:T(8,128)(2,1)} %bitcast.7) | data formatting | bytes 11796480 | tf_op jit(solution)/shard_map/all_to_all | solution.py:78
  218.2 3.9 copy.37
  222.0 1.7 fusion.455
  223.7 0.2 slice.55
  223.9 1.4 copy-done.1
  225.3 1.7 copy.61
  227.0 0.0 copy-start.11
  227.1 6.2 %fusion.108 = f32[2,6,256,384]{3,2,1,0:T(8,128)S(1)} fusion(bf16[1,5,6,384,256]{4,3,2,1,0:T(8,128)(2,1)} %bitcast.123, s32[384]{0:T(512)S(1)} %get-tuple-element.20, s32[384]{0:T(512)S(1)} %get-tuple-element.21, s32[384]{0:T(512)S(1)} %get-tuple-element.22, s32[384]{0:T(512)} %get-tuple-element.23, pred[384]{0:T(512)(128)(4,1)} %get-tuple-element.27, ...), kind=kOutput, calls=%fused_computation.131 | convolution fusion | flops 922042368 | bytes 7086592 | tf_op jit(solution)/shard_map/ij,sczjx->sczix/dot_general | solution.py:53
  233.3 0.0 copy-done.4
  233.3 0.0 copy-done.11
  233.3 0.0 copy-done.12
  233.3 0.0 copy-done.13
  233.4 0.0 copy-done.14
  233.4 0.0 copy-done.15
  233.4 6.4 %fusion = f32[1,2,6,384,256]{3,4,2,1,0:T(8,128)S(1)} fusion(f32[2,6,256,384]{3,2,1,0:T(8,128)S(1)} %fusion.108, f32[384]{0:T(512)S(1)} %copy-done.11, bf16[1,5,6,384,256]{4,3,2,1,0:T(8,128)(2,1)} %bitcast.124, s32[384]{0:T(512)S(1)} %get-tuple-element.20, pred[384]{0:T(512)(128)(4,1)S(1)} %copy-done.15, s32[384]{0:T(512)S(1)} %get-tuple-element.21, ...), kind=kOutput, calls=%fused_computation.15 | convolution fusion | flops 923959296 | bytes 11805696 | tf_op jit(solution)/shard_map/ij,sczjx->sczix/dot_general | solution.py:52
  239.8 1.2 slice.94
  240.9 1.4 fusion.107
  242.3 1.6 copy.41
  243.9 2.4 copy.40
  246.2 4.8 pad_maximum_fusion.1
  251.0 6.2 %copy.42 = bf16[1,5,6,384,256]{4,2,1,0,3:T(8,128)(2,1)S(1)} copy(bf16[1,5,6,384,256]{4,3,2,1,0:T(8,128)(2,1)} %pad_maximum_fusion.1) | data formatting | bytes 11796480 | tf_op jit(solution)/shard_map/stack | solution.py:85
  257.2 183.2 %all_to_all.41 = bf16[1,5,6,384,256]{4,2,1,0,3:T(8,128)(2,1)} all-to-all(bf16[1,5,6,384,256]{4,2,1,0,3:T(8,128)(2,1)S(1)} %copy.42), channel_id=1, replica_groups=mesh['snap'=8,'py'=4,'pz'=8] {'snap'}, dimensions={3} | all-to-all | bytes 11796480 | tf_op jit(solution)/shard_map/all_to_all | solution.py:87
  440.4 4.6 copy.43
  445.1 0.1 fusion.144
  445.2 0.3 fusion.143
  445.5 0.3 fusion.142
  445.9 0.3 fusion.141
  446.1 0.1 fusion.140
  446.2 0.3 fusion.139
  446.5 0.3 fusion.138
  446.9 0.2 fusion.137
  447.1 5.1 copy.44
  452.2 7.5 %all-to-all-start.2 = ((bf16[8,8,5,6,6,256]{5,1,4,3,2,0:T(8,128)(2,1)}), bf16[8,8,5,6,6,256]{5,1,4,3,2,0:T(8,128)(2,1)}, u32[]{:S(2)}, u32[]{:S(2)}) async-start(bf16[8,8,5,6,6,256]{5,1,4,3,2,0:T(8,128)(2,1)} %copy.44), calls=%async_computation.2 | async-start | bytes 11796480 | tf_op jit(solution)/shard_map/all_to_all | solution.py:12
  459.7 81.9 %all-to-all-done.2 = bf16[8,8,5,6,6,256]{5,1,4,3,2,0:T(8,128)(2,1)} async-done(((bf16[8,8,5,6,6,256]{5,1,4,3,2,0:T(8,128)(2,1)}), bf16[8,8,5,6,6,256]{5,1,4,3,2,0:T(8,128)(2,1)}, u32[]{:S(2)}, u32[]{:S(2)}) %all-to-all-start.2) | async-done | bytes 5898272 | tf_op jit(solution)/shard_map/all_to_all | solution.py:12
  541.7 3.2 copy.45
  544.9 0.2 slice.61
  545.0 0.2 fusion.454
  545.3 0.4 copy.65
  545.7 0.0 copy-start.9
  545.7 2.1 fusion.123
  547.8 2.2 multiply_bitcast_fusion
  550.0 1.3 fusion.106
  551.3 0.4 pad_maximum_fusion.2
  551.8 0.0 copy-done
  551.8 4.0 fusion.130
  555.8 2.9 copy.51
  (23 shorter events, 0.1 us)
Async XLA Ops:
  0.0 551.8 %copy-start = (f32[8,4]{0,1:T(4,128)S(1)}, f32[8,4]{0,1:T(4,128)}, u32[]{:S(2)}) copy-start(f32[8,4]{0,1:T(4,128)} %param.10) | copy-start | bytes 388
  1.8 8.1 %copy-start.2 = (bf16[1,3,6,96,1024]{4,3,2,1,0:T(8,128)(2,1)S(1)}, bf16[1,3,6,96,1024]{4,3,2,1,0:T(8,128)(2,1)}, u32[]{:S(2)}) copy-start(bf16[1,3,6,96,1024]{4,3,2,1,0:T(8,128)(2,1)} %param.6) | copy-start | bytes 10616836
  9.9 29.3 %copy-start.3 = (s32[1024]{0:T(1024)S(1)}, s32[1024]{0:T(1024)}, u32[]{:S(2)}) copy-start(s32[1024]{0:T(1024)} %get-tuple-element.15) | copy-start | bytes 12292
  9.9 29.3 %copy-start.5 = (pred[1024]{0:T(1024)(128)(4,1)S(1)}, pred[1024]{0:T(1024)(128)(4,1)}, u32[]{:S(2)}) copy-start(pred[1024]{0:T(1024)(128)(4,1)} %get-tuple-element.16) | copy-start | bytes 3076
  9.9 29.4 %copy-start.6 = (pred[1024]{0:T(1024)(128)(4,1)S(1)}, pred[1024]{0:T(1024)(128)(4,1)}, u32[]{:S(2)}) copy-start(pred[1024]{0:T(1024)(128)(4,1)} %get-tuple-element.17) | copy-start | bytes 3076
  9.9 29.4 %copy-start.7 = (pred[1024]{0:T(1024)(128)(4,1)S(1)}, pred[1024]{0:T(1024)(128)(4,1)}, u32[]{:S(2)}) copy-start(pred[1024]{0:T(1024)(128)(4,1)} %get-tuple-element.18) | copy-start | bytes 3076
  9.9 29.4 %copy-start.8 = (pred[1024]{0:T(1024)(128)(4,1)S(1)}, pred[1024]{0:T(1024)(128)(4,1)}, u32[]{:S(2)}) copy-start(pred[1024]{0:T(1024)(128)(4,1)} %get-tuple-element.19) | copy-start | bytes 3076
  10.0 29.4 %copy-start.10 = (f32[1024]{0:T(1024)S(1)}, f32[1024]{0:T(1024)}, u32[]{:S(2)}) copy-start(f32[1024]{0:T(1024)} %param.7) | copy-start | bytes 12292
  85.0 120.8 %all-to-all-start = ((bf16[1,5,6,96,1024]{3,2,1,0,4:T(8,128)(2,1)}), bf16[1,5,6,96,1024]{3,2,1,0,4:T(8,128)(2,1)}, u32[]{:S(2)}, u32[]{:S(2)}) async-start(bf16[1,5,6,96,1024]{3,2,1,0,4:T(8,128)(2,1)} %pad_maximum_fusion), calls=%async_computation | async-start | bytes 20971520 | tf_op jit(solution)/shard_map/all_to_all | solution.py:78
  222.0 3.3 copy-start.1
  227.0 6.3 %copy-start.4 = (s32[384]{0:T(512)S(1)}, s32[384]{0:T(512)}, u32[]{:S(2)}) copy-start(s32[384]{0:T(512)} %get-tuple-element.23) | copy-start | bytes 4612
  227.0 6.3 %copy-start.11 = (f32[384]{0:T(512)S(1)}, f32[384]{0:T(512)}, u32[]{:S(2)}) copy-start(f32[384]{0:T(512)} %param.8) | copy-start | bytes 4612
  227.0 6.3 %copy-start.12 = (pred[384]{0:T(512)(128)(4,1)S(1)}, pred[384]{0:T(512)(128)(4,1)}, u32[]{:S(2)}) copy-start(pred[384]{0:T(512)(128)(4,1)} %get-tuple-element.24) | copy-start | bytes 1156
  227.0 6.3 %copy-start.13 = (pred[384]{0:T(512)(128)(4,1)S(1)}, pred[384]{0:T(512)(128)(4,1)}, u32[]{:S(2)}) copy-start(pred[384]{0:T(512)(128)(4,1)} %get-tuple-element.25) | copy-start | bytes 1156
  227.0 6.3 %copy-start.14 = (pred[384]{0:T(512)(128)(4,1)S(1)}, pred[384]{0:T(512)(128)(4,1)}, u32[]{:S(2)}) copy-start(pred[384]{0:T(512)(128)(4,1)} %get-tuple-element.26) | copy-start | bytes 1156
  227.0 6.3 %copy-start.15 = (pred[384]{0:T(512)(128)(4,1)S(1)}, pred[384]{0:T(512)(128)(4,1)}, u32[]{:S(2)}) copy-start(pred[384]{0:T(512)(128)(4,1)} %get-tuple-element.27) | copy-start | bytes 1156
  452.2 89.5 %all-to-all-start.2 = ((bf16[8,8,5,6,6,256]{5,1,4,3,2,0:T(8,128)(2,1)}), bf16[8,8,5,6,6,256]{5,1,4,3,2,0:T(8,128)(2,1)}, u32[]{:S(2)}, u32[]{:S(2)}) async-start(bf16[8,8,5,6,6,256]{5,1,4,3,2,0:T(8,128)(2,1)} %copy.44), calls=%async_computation.2 | async-start | bytes 11796480 | tf_op jit(solution)/shard_map/all_to_all | solution.py:12
  545.7 2.2 copy-start.9
